TPU v7x, 1024 devices: a whole 4x8x16 slice. The times are simulated.
1024 devices in a mesh: row: 32 (over z_lo, x, core), col: 32 (over z_hi, y).
Axes of the slice: x: 4, y: 8, z: 16 (z_hi: 4, z_lo: 4; z = z_hi * 4 + z_lo), core: 2. Of those that a mesh axis runs over, the one named last changes fastest.
Arguments:
- obj: float32 [2, 2, 4096, 4096], P(None, None, 'row', 'col'), may hold values from -4 to 4
- bank: bfloat16 [8, 2, 128, 128], replicated, may hold values from -0.21875 to 0.21875
- band_index: int32 [2, 2, 3], replicated, may hold values from 0 to 7
- tilt: int32 [2, 2], replicated, may hold values from -24 to 23
- tile_shift: int32 [2, 2], replicated, may hold values from 0 to 7
- slice_order: int32 [2], replicated, may hold values from 0 to 1, each once
- cot: bfloat16 [2, 2, 4096, 4096], P(None, None, 'row', 'col'), may hold values from -6 to 6
Outputs:
- exit_field: bfloat16 [2, 2, 4096, 4096], P(None, None, 'row', 'col')
- grad_obj: float32 [2, 2, 4096, 4096], P(None, None, 'row', 'col')
All inputs are finite; a program needn't handle non-finite values.
Results may differ from a plain program's by a relative error of at most 0.014.
Values may be sent and summed in bfloat16 or wider, within the bound.
A program may use at most 32 MiB of HBM per device.

v0:
```python
import math

import jax
import jax.numpy as jnp
from jax import lax
from jax.sharding import PartitionSpec as P


def with_halo(block, sides, width):
    for axis, dim in sides:
        count = lax.axis_size(axis)
        forward = [(i, i + 1) for i in range(count - 1)]
        forward.append((count - 1, 0))
        backward = [(target, source) for source, target in forward]
        low = lax.ppermute(
            lax.slice_in_dim(block, block.shape[dim] - width, None, axis=dim), axis, forward
        )
        high = lax.ppermute(lax.slice_in_dim(block, 0, width, axis=dim), axis, backward)
        block = jnp.concatenate([low, block, high], axis=dim)
    return block


def from_behind(block, axis, distance):
    devices = range(lax.axis_size(axis))
    route = [((i - distance) % len(devices), i) for i in devices]
    return lax.ppermute(block, axis, route)


def incident(tilt_row, tilt_col, row_start, col_start, rows, cols, total_rows, total_cols):
    row_ids = row_start + jnp.arange(rows, dtype=jnp.int32)
    col_ids = col_start + jnp.arange(cols, dtype=jnp.int32)
    row_phase = jnp.mod(tilt_row * row_ids, total_rows).astype(jnp.float32) / total_rows
    col_phase = jnp.mod(tilt_col * col_ids, total_cols).astype(jnp.float32) / total_cols
    phase = 2.0 * math.pi * (row_phase[:, None] + col_phase[None, :])
    return jnp.stack([jnp.cos(phase), jnp.sin(phase)]).astype(jnp.bfloat16)


def rows_product(matrix, field, width, adjoint):
    lead, rows, cols = field.shape
    blocks = field.reshape(lead, rows // width, width, cols)
    form = "qp,anqc->anpc" if adjoint else "pq,anqc->anpc"
    return jnp.einsum(form, matrix, blocks, preferred_element_type=jnp.float32).reshape(
        lead, rows, cols
    )


def cols_product(matrix, field, width, adjoint):
    lead, rows, cols = field.shape
    blocks = field.reshape(lead, rows, cols // width, width)
    form = "arnq,pq->arnp" if adjoint else "arnq,qp->arnp"
    return jnp.einsum(form, blocks, matrix, preferred_element_type=jnp.float32).reshape(
        lead, rows, cols
    )


def band_apply(padded, mats, length, axis, adjoint):
    width = mats[0][0].shape[0]
    total_real = None
    total_imag = None
    for position in range(3):
        offset = position - 1
        start = width * (1 - offset) if adjoint else width * (1 + offset)
        segment = lax.slice_in_dim(padded, start, start + length, axis=axis)
        real_in = segment[:, 0]
        imag_in = segment[:, 1]
        mat_real = mats[position][0]
        mat_imag = mats[position][1]
        if axis == 2:
            product = rows_product
        else:
            product = cols_product
        if adjoint:
            part_real = product(mat_real, real_in, width, True) + product(
                mat_imag, imag_in, width, True
            )
            part_imag = product(mat_real, imag_in, width, True) - product(
                mat_imag, real_in, width, True
            )
        else:
            part_real = product(mat_real, real_in, width, False) - product(
                mat_imag, imag_in, width, False
            )
            part_imag = product(mat_real, imag_in, width, False) + product(
                mat_imag, real_in, width, False
            )
        total_real = part_real if total_real is None else total_real + part_real
        total_imag = part_imag if total_imag is None else total_imag + part_imag
    return jnp.stack([total_real, total_imag], axis=1).astype(jnp.bfloat16)


def transmit(trans, field):
    field_real = field[:, 0].astype(jnp.float32)
    field_imag = field[:, 1].astype(jnp.float32)
    out_real = trans[0] * field_real - trans[1] * field_imag
    out_imag = trans[0] * field_imag + trans[1] * field_real
    return jnp.stack([out_real, out_imag], axis=1).astype(jnp.bfloat16)


def rim_rows(field, width):
    return with_halo(field, (("row", 2),), width)


def rim_cols(field, width):
    return with_halo(field, (("col", 3),), width)


def move_tiles(field, row_steps, col_steps, direction):
    shift_count = min(8, min(lax.axis_size("row"), lax.axis_size("col")))
    bit_total = (shift_count - 1).bit_length()
    for bit_number in range(bit_total):
        moved = from_behind(field, "row", direction * (1 << bit_number))
        taken = row_steps // (1 << bit_number) % 2 == 1
        field = jnp.where(taken[:, None, None, None], moved, field)
    for bit_number in range(bit_total):
        moved = from_behind(field, "col", direction * (1 << bit_number))
        taken = col_steps // (1 << bit_number) % 2 == 1
        field = jnp.where(taken[:, None, None, None], moved, field)
    return field


def local(obj, bank, band_index, tilt, tile_shift, slice_order, cot):
    width = bank.shape[2]
    angles = cot.shape[0]
    rows = cot.shape[2]
    cols = cot.shape[3]
    layers = obj.shape[0]
    total_rows = rows * lax.axis_size("row")
    total_cols = cols * lax.axis_size("col")
    row_start = lax.axis_index("row") * rows
    col_start = lax.axis_index("col") * cols
    field = jnp.stack(
        [
            incident(
                tilt[angle, 0],
                tilt[angle, 1],
                row_start,
                col_start,
                rows,
                cols,
                total_rows,
                total_cols,
            )
            for angle in range(angles)
        ]
    )
    saved = []
    all_row_mats = []
    all_col_mats = []
    for layer in range(layers):
        saved.append(field)
        trans = obj[slice_order[layer]]
        field = transmit(trans, field)
        row_mats = [
            (bank[band_index[layer, 0, p], 0], bank[band_index[layer, 0, p], 1]) for p in range(3)
        ]
        col_mats = [
            (bank[band_index[layer, 1, p], 0], bank[band_index[layer, 1, p], 1]) for p in range(3)
        ]
        all_row_mats.append(row_mats)
        all_col_mats.append(col_mats)
        field = band_apply(rim_rows(field, width), row_mats, rows, 2, False)
        field = band_apply(rim_cols(field, width), col_mats, cols, 3, False)
    exit_field = move_tiles(field, tile_shift[:, 0], tile_shift[:, 1], 1)
    grad_field = move_tiles(cot, tile_shift[:, 0], tile_shift[:, 1], -1)
    grad = jnp.zeros(obj.shape, jnp.float32)
    for layer in range(layers - 1, -1, -1):
        back_cols = band_apply(rim_cols(grad_field, width), all_col_mats[layer], cols, 3, True)
        back_rows = band_apply(rim_rows(back_cols, width), all_row_mats[layer], rows, 2, True)
        grad_real = back_rows[:, 0].astype(jnp.float32)
        grad_imag = back_rows[:, 1].astype(jnp.float32)
        psi_real = saved[layer][:, 0].astype(jnp.float32)
        psi_imag = saved[layer][:, 1].astype(jnp.float32)
        term_real = jnp.sum(grad_real * psi_real + grad_imag * psi_imag, axis=0)
        term_imag = jnp.sum(grad_imag * psi_real - grad_real * psi_imag, axis=0)
        grad = grad.at[slice_order[layer]].add(jnp.stack([term_real, term_imag]))
        if layer > 0:
            trans = obj[slice_order[layer]]
            new_real = grad_real * trans[0] + grad_imag * trans[1]
            new_imag = grad_imag * trans[0] - grad_real * trans[1]
            grad_field = jnp.stack([new_real, new_imag], axis=1).astype(jnp.bfloat16)
    return (exit_field, grad)


def solution(mesh):
    in_specs = (P(None, None, "row", "col"), P(), P(), P(), P(), P(), P(None, None, "row", "col"))
    out_specs = (P(None, None, "row", "col"), P(None, None, "row", "col"))
    return jax.shard_map(local, mesh=mesh, in_specs=in_specs, out_specs=out_specs, check_vma=False)
```

profile of v0, /device:TPU:4, one launch (start us, length us, event | category | flops | bytes accessed | tf_op | source)
XLA Modules:
  0.0 318.3 jit_solution(10266836413433920508)
XLA Ops:
  0.7 0.7 copy-done.5
  1.4 0.6 fusion.507
  4.6 0.6 fusion.506
  6.5 1.0 dynamic-slice_bitcast_fusion.3
  7.7 1.3 fusion.490
  9.0 0.3 fusion.139
  9.3 1.3 fusion.494
  10.7 0.3 fusion.141
  11.1 2.1 collective-permute-start.1
  13.1 2.4 collective-permute-start
  15.6 3.2 collective-permute-start.14
  18.8 0.7 fusion.505
  22.0 0.5 copy-done.3
  43.8 0.6 copy-done.6
  44.5 0.7 and_reduce_fusion
  46.6 21.1 %collective-permute-start.3 = (bf16[2,2,128,128]{2,3,0,1:T(8,128)(2,1)S(1)}, bf16[2,2,128,128]{2,3,0,1:T(8,128)(2,1)S(1)}, u32[]{:S(2)}, u32[]{:S(2)}) collective-permute-start(bf16[2,2,128,128]{2,3,0,1:T(8,128)(2,1)S(1)} %pad_maximum_fusion.1), channel_id=1, source_target_pairs={{1,0},{2,1},{3,2},{4,3},{5,4},{6,5},{7,6},{8,7},{9,8},{10,9},{11,1... | collective-permute-start | bytes 393224 | tf_op jit(solution)/shard_map/ppermute | solution.py:18
  67.7 1.9 collective-permute-start.2
  70.3 2.4 collective-permute-start.15
  73.0 5.5 %collective-permute-done.15 = bf16[2,2,128,128]{3,2,0,1:T(8,128)(2,1)S(1)} collective-permute-done((bf16[2,2,128,128]{3,2,0,1:T(8,128)(2,1)S(1)}, bf16[2,2,128,128]{3,2,0,1:T(8,128)(2,1)S(1)}, u32[]{:S(2)}, u32[]{:S(2)}) %collective-permute-start.15) | collective-permute-done | bytes 131104 | tf_op jit(solution)/shard_map/ppermute | solution.py:26
  78.5 10.0 %collective-permute-start.16 = (bf16[2,2,128,128]{3,2,0,1:T(8,128)(2,1)S(1)}, bf16[2,2,128,128]{3,2,0,1:T(8,128)(2,1)S(1)}, u32[]{:S(2)}, u32[]{:S(2)}) collective-permute-start(bf16[2,2,128,128]{3,2,0,1:T(8,128)(2,1)S(1)} %broadcast_select_fusion.2), channel_id=1, source_target_pairs={{128,0},{160,32},{192,64},{224,96},{256,128},{288,160},{320,192},{... | collective-permute-start | bytes 393224 | tf_op jit(solution)/shard_map/ppermute | solution.py:26
  89.5 1.5 collective-permute-done.16
  91.1 10.1 %collective-permute-start.17 = (bf16[2,2,128,128]{3,2,0,1:T(8,128)(2,1)S(1)}, bf16[2,2,128,128]{3,2,0,1:T(8,128)(2,1)S(1)}, u32[]{:S(2)}, u32[]{:S(2)}) collective-permute-start(bf16[2,2,128,128]{3,2,0,1:T(8,128)(2,1)S(1)} %broadcast_select_fusion.4), channel_id=1, source_target_pairs={{1,0},{2,1},{3,2},{4,3},{5,4},{6,5},{7,6},{8,7},{9,8},{10,9},{11,1... | collective-permute-start | bytes 393224 | tf_op jit(solution)/shard_map/ppermute | solution.py:26
  101.4 10.2 %collective-permute-done.17 = bf16[2,2,128,128]{3,2,0,1:T(8,128)(2,1)S(1)} collective-permute-done((bf16[2,2,128,128]{3,2,0,1:T(8,128)(2,1)S(1)}, bf16[2,2,128,128]{3,2,0,1:T(8,128)(2,1)S(1)}, u32[]{:S(2)}, u32[]{:S(2)}) %collective-permute-start.17) | collective-permute-done | bytes 131104 | tf_op jit(solution)/shard_map/ppermute | solution.py:26
  111.8 1.9 collective-permute-start.18
  113.9 6.6 %collective-permute-done.18 = bf16[2,2,128,128]{3,2,0,1:T(8,128)(2,1)S(1)} collective-permute-done((bf16[2,2,128,128]{3,2,0,1:T(8,128)(2,1)S(1)}, bf16[2,2,128,128]{3,2,0,1:T(8,128)(2,1)S(1)}, u32[]{:S(2)}, u32[]{:S(2)}) %collective-permute-start.18) | collective-permute-done | bytes 131104 | tf_op jit(solution)/shard_map/ppermute | solution.py:26
  120.5 1.9 collective-permute-start.19
  122.7 10.7 %collective-permute-done.19 = bf16[2,2,128,128]{3,2,0,1:T(8,128)(2,1)S(1)} collective-permute-done((bf16[2,2,128,128]{3,2,0,1:T(8,128)(2,1)S(1)}, bf16[2,2,128,128]{3,2,0,1:T(8,128)(2,1)S(1)}, u32[]{:S(2)}, u32[]{:S(2)}) %collective-permute-start.19) | collective-permute-done | bytes 131104 | tf_op jit(solution)/shard_map/ppermute | solution.py:26
  133.4 10.5 %collective-permute-start.21 = (bf16[2,2,128,128]{3,2,0,1:T(8,128)(2,1)S(1)}, bf16[2,2,128,128]{3,2,0,1:T(8,128)(2,1)S(1)}, u32[]{:S(2)}, u32[]{:S(2)}) collective-permute-start(bf16[2,2,128,128]{3,2,0,1:T(8,128)(2,1)S(1)} %broadcast_select_fusion.10), channel_id=1, source_target_pairs={{0,1},{1,2},{2,3},{3,4},{4,5},{5,6},{6,7},{7,8},{8,9},{9,10},{10,1... | collective-permute-start | bytes 393224 | tf_op jit(solution)/shard_map/ppermute | solution.py:15
  144.0 12.9 %collective-permute-start.20 = (bf16[2,2,128,128]{3,2,0,1:T(8,128)(2,1)S(1)}, bf16[2,2,128,128]{3,2,0,1:T(8,128)(2,1)S(1)}, u32[]{:S(2)}, u32[]{:S(2)}) collective-permute-start(bf16[2,2,128,128]{3,2,0,1:T(8,128)(2,1)S(1)} %broadcast_select_fusion.10), channel_id=1, source_target_pairs={{1,0},{2,1},{3,2},{4,3},{5,4},{6,5},{7,6},{8,7},{9,8},{10,9},{11,1... | collective-permute-start | bytes 393224 | tf_op jit(solution)/shard_map/ppermute | solution.py:18
  157.6 0.4 collective-permute-done.21
  158.3 1.1 collective-permute-done.20
  160.9 1.9 collective-permute-start.23
  162.9 3.6 %collective-permute-start.22 = (bf16[2,2,128,128]{3,2,0,1:T(8,128)(2,1)S(1)}, bf16[2,2,128,128]{3,2,0,1:T(8,128)(2,1)S(1)}, u32[]{:S(2)}, u32[]{:S(2)}) collective-permute-start(bf16[2,2,128,128]{3,2,0,1:T(8,128)(2,1)S(1)} %pad_maximum_fusion.5), channel_id=1, source_target_pairs={{32,0},{64,32},{96,64},{128,96},{160,128},{192,160},{224,192},{256... | collective-permute-start | bytes 393224 | tf_op jit(solution)/shard_map/ppermute | solution.py:18
  167.0 0.2 collective-permute-done.23
  167.7 1.3 collective-permute-done.22
  170.1 0.3 add_convert_fusion
  170.6 1.9 collective-permute-start.25
  172.5 10.4 %collective-permute-start.24 = (bf16[2,2,128,128]{3,2,0,1:T(8,128)(2,1)S(1)}, bf16[2,2,128,128]{3,2,0,1:T(8,128)(2,1)S(1)}, u32[]{:S(2)}, u32[]{:S(2)}) collective-permute-start(bf16[2,2,128,128]{3,2,0,1:T(8,128)(2,1)S(1)} %pad_maximum_fusion.6), channel_id=1, source_target_pairs={{1,0},{2,1},{3,2},{4,3},{5,4},{6,5},{7,6},{8,7},{9,8},{10,9},{11,1... | collective-permute-start | bytes 393224 | tf_op jit(solution)/shard_map/ppermute | solution.py:18
  183.3 3.8 %collective-permute-start.5 = (bf16[2,2,128,128]{3,2,0,1:T(8,128)(2,1)S(1)}, bf16[2,2,128,128]{3,2,0,1:T(8,128)(2,1)S(1)}, u32[]{:S(2)}, u32[]{:S(2)}) collective-permute-start(bf16[2,2,128,128]{3,2,0,1:T(8,128)(2,1)S(1)} %pad_maximum_fusion.2), channel_id=1, source_target_pairs={{32,0},{64,32},{96,64},{128,96},{160,128},{192,160},{224,192},{256... | collective-permute-start | bytes 393224 | tf_op jit(solution)/shard_map/ppermute | solution.py:18
  187.1 1.9 collective-permute-start.4
  190.0 0.7 maximum_select_fusion
  191.2 3.0 collective-permute-done.24
  195.3 2.2 collective-permute-start.27
  197.5 3.8 %collective-permute-start.26 = (bf16[2,2,128,128]{3,2,0,1:T(8,128)(2,1)S(1)}, bf16[2,2,128,128]{3,2,0,1:T(8,128)(2,1)S(1)}, u32[]{:S(2)}, u32[]{:S(2)}) collective-permute-start(bf16[2,2,128,128]{3,2,0,1:T(8,128)(2,1)S(1)} %pad_maximum_fusion.7), channel_id=1, source_target_pairs={{32,0},{64,32},{96,64},{128,96},{160,128},{192,160},{224,192},{256... | collective-permute-start | bytes 393224 | tf_op jit(solution)/shard_map/ppermute | solution.py:18
  203.5 10.4 %collective-permute-start.7 = (bf16[2,2,128,128]{2,3,0,1:T(8,128)(2,1)S(1)}, bf16[2,2,128,128]{2,3,0,1:T(8,128)(2,1)S(1)}, u32[]{:S(2)}, u32[]{:S(2)}) collective-permute-start(bf16[2,2,128,128]{2,3,0,1:T(8,128)(2,1)S(1)} %pad_maximum_fusion.3), channel_id=1, source_target_pairs={{1,0},{2,1},{3,2},{4,3},{5,4},{6,5},{7,6},{8,7},{9,8},{10,9},{11,1... | collective-permute-start | bytes 393224 | tf_op jit(solution)/shard_map/ppermute | solution.py:18
  213.9 1.9 collective-permute-start.6
  216.8 2.5 collective-permute-done.7
  219.8 9.5 %collective-permute-done.6 = bf16[2,2,128,128]{2,3,0,1:T(8,128)(2,1)S(1)} collective-permute-done((bf16[2,2,128,128]{2,3,0,1:T(8,128)(2,1)S(1)}, bf16[2,2,128,128]{2,3,0,1:T(8,128)(2,1)S(1)}, u32[]{:S(2)}, u32[]{:S(2)}) %collective-permute-start.6) | collective-permute-done | bytes 131104 | tf_op jit(solution)/shard_map/ppermute | solution.py:15
  230.5 1.9 collective-permute-start.8
  233.0 3.8 %collective-permute-done.8 = bf16[2,2,128,128]{3,2,0,1:T(8,128)(2,1)S(1)} collective-permute-done((bf16[2,2,128,128]{3,2,0,1:T(8,128)(2,1)S(1)}, bf16[2,2,128,128]{3,2,0,1:T(8,128)(2,1)S(1)}, u32[]{:S(2)}, u32[]{:S(2)}) %collective-permute-start.8) | collective-permute-done | bytes 131104 | tf_op jit(solution)/shard_map/ppermute | solution.py:26
  236.8 6.3 %collective-permute-start.9 = (bf16[2,2,128,128]{3,2,0,1:T(8,128)(2,1)S(1)}, bf16[2,2,128,128]{3,2,0,1:T(8,128)(2,1)S(1)}, u32[]{:S(2)}, u32[]{:S(2)}) collective-permute-start(bf16[2,2,128,128]{3,2,0,1:T(8,128)(2,1)S(1)} %broadcast_select_fusion.1), channel_id=1, source_target_pairs={{960,0},{992,32},{0,64},{32,96},{64,128},{96,160},{128,192},{160,2... | collective-permute-start | bytes 393224 | tf_op jit(solution)/shard_map/ppermute | solution.py:26
  243.4 2.3 collective-permute-done.9
  245.8 5.3 %collective-permute-start.10 = (bf16[2,2,128,128]{3,2,0,1:T(8,128)(2,1)S(1)}, bf16[2,2,128,128]{3,2,0,1:T(8,128)(2,1)S(1)}, u32[]{:S(2)}, u32[]{:S(2)}) collective-permute-start(bf16[2,2,128,128]{3,2,0,1:T(8,128)(2,1)S(1)} %broadcast_select_fusion.3), channel_id=1, source_target_pairs={{896,0},{928,32},{960,64},{992,96},{0,128},{32,160},{64,192},{96,2... | collective-permute-start | bytes 393224 | tf_op jit(solution)/shard_map/ppermute | solution.py:26
  251.3 15.9 %collective-permute-done.10 = bf16[2,2,128,128]{3,2,0,1:T(8,128)(2,1)S(1)} collective-permute-done((bf16[2,2,128,128]{3,2,0,1:T(8,128)(2,1)S(1)}, bf16[2,2,128,128]{3,2,0,1:T(8,128)(2,1)S(1)}, u32[]{:S(2)}, u32[]{:S(2)}) %collective-permute-start.10) | collective-permute-done | bytes 131104 | tf_op jit(solution)/shard_map/ppermute | solution.py:26
  267.3 1.9 collective-permute-start.11
  269.4 18.6 %collective-permute-done.11 = bf16[2,2,128,128]{3,2,0,1:T(8,128)(2,1)S(1)} collective-permute-done((bf16[2,2,128,128]{3,2,0,1:T(8,128)(2,1)S(1)}, bf16[2,2,128,128]{3,2,0,1:T(8,128)(2,1)S(1)}, u32[]{:S(2)}, u32[]{:S(2)}) %collective-permute-start.11) | collective-permute-done | bytes 131104 | tf_op jit(solution)/shard_map/ppermute | solution.py:26
  288.1 1.9 collective-permute-start.12
  290.2 11.7 %collective-permute-done.12 = bf16[2,2,128,128]{3,2,0,1:T(8,128)(2,1)S(1)} collective-permute-done((bf16[2,2,128,128]{3,2,0,1:T(8,128)(2,1)S(1)}, bf16[2,2,128,128]{3,2,0,1:T(8,128)(2,1)S(1)}, u32[]{:S(2)}, u32[]{:S(2)}) %collective-permute-start.12) | collective-permute-done | bytes 131104 | tf_op jit(solution)/shard_map/ppermute | solution.py:26
  301.9 1.9 collective-permute-start.13
  303.9 0.2 fusion.72
  304.1 0.7 fusion.66
  304.8 0.8 copy.248
  305.6 11.9 %collective-permute-done.13 = bf16[2,2,128,128]{3,2,0,1:T(8,128)(2,1)S(1)} collective-permute-done((bf16[2,2,128,128]{3,2,0,1:T(8,128)(2,1)S(1)}, bf16[2,2,128,128]{3,2,0,1:T(8,128)(2,1)S(1)}, u32[]{:S(2)}, u32[]{:S(2)}) %collective-permute-start.13) | collective-permute-done | bytes 131104 | tf_op jit(solution)/shard_map/ppermute | solution.py:26
  317.6 0.7 copy.247
  (147 shorter events, 19.4 us)
Async XLA Ops:
  0.6 20.7 %copy-start = (bf16[8,2,128,128]{3,2,1,0:T(8,128)(2,1)S(1)}, bf16[8,2,128,128]{3,2,1,0:T(8,128)(2,1)}, u32[]{:S(2)}) copy-start(bf16[8,2,128,128]{3,2,1,0:T(8,128)(2,1)} %param.12) | copy-start | bytes 1572868
  0.6 0.7 copy-start.5
  3.9 0.7 copy-start.4
  11.1 4.5 %copy-start.1 = (bf16[2,2,128,128]{3,2,1,0:T(8,128)(2,1)S(1)}, bf16[2,2,128,128]{3,2,1,0:T(8,128)(2,1)}, u32[]{:S(2)}) copy-start(bf16[2,2,128,128]{3,2,1,0:T(8,128)(2,1)} %param.17) | copy-start | bytes 393220
  11.1 34.1 %collective-permute-start.1 = (bf16[2,2,128,128]{2,3,0,1:T(8,128)(2,1)S(1)}, bf16[2,2,128,128]{2,3,0,1:T(8,128)(2,1)S(1)}, u32[]{:S(2)}, u32[]{:S(2)}) collective-permute-start(bf16[2,2,128,128]{2,3,0,1:T(8,128)(2,1)S(1)} %pad_maximum_fusion), channel_id=1, source_target_pairs={{32,0},{64,32},{96,64},{128,96},{160,128},{192,160},{224,192},{256... | collective-permute-start | bytes 393224 | tf_op jit(solution)/shard_map/ppermute | solution.py:18
  13.1 32.4 %collective-permute-start = (bf16[2,2,128,128]{2,3,0,1:T(8,128)(2,1)S(1)}, bf16[2,2,128,128]{2,3,0,1:T(8,128)(2,1)S(1)}, u32[]{:S(2)}, u32[]{:S(2)}) collective-permute-start(bf16[2,2,128,128]{2,3,0,1:T(8,128)(2,1)S(1)} %pad_maximum_fusion), channel_id=1, source_target_pairs={{0,32},{32,64},{64,96},{96,128},{128,160},{160,192},{192,224},{224... | collective-permute-start | bytes 393224 | tf_op jit(solution)/shard_map/ppermute | solution.py:15
  15.6 3.2 %copy-start.2 = (s32[2,2,3]{2,1,0:T(2,128)S(1)}, s32[2,2,3]{2,1,0:T(2,128)}, u32[]{:S(2)}) copy-start(s32[2,2,3]{2,1,0:T(2,128)} %param.13) | copy-start | bytes 148
  15.6 54.6 %collective-permute-start.14 = (bf16[2,2,128,128]{3,2,0,1:T(8,128)(2,1)S(1)}, bf16[2,2,128,128]{3,2,0,1:T(8,128)(2,1)S(1)}, u32[]{:S(2)}, u32[]{:S(2)}) collective-permute-start(bf16[2,2,128,128]{3,2,0,1:T(8,128)(2,1)S(1)} %copy.208), channel_id=1, source_target_pairs={{32,0},{64,32},{96,64},{128,96},{160,128},{192,160},{224,192},{256... | collective-permute-start | bytes 393224 | tf_op jit(solution)/shard_map/ppermute | solution.py:26
  21.8 0.7 copy-start.3
  43.8 0.7 copy-start.6
  46.6 41.9 %collective-permute-start.3 = (bf16[2,2,128,128]{2,3,0,1:T(8,128)(2,1)S(1)}, bf16[2,2,128,128]{2,3,0,1:T(8,128)(2,1)S(1)}, u32[]{:S(2)}, u32[]{:S(2)}) collective-permute-start(bf16[2,2,128,128]{2,3,0,1:T(8,128)(2,1)S(1)} %pad_maximum_fusion.1), channel_id=1, source_target_pairs={{1,0},{2,1},{3,2},{4,3},{5,4},{6,5},{7,6},{8,7},{9,8},{10,9},{11,1... | collective-permute-start | bytes 393224 | tf_op jit(solution)/shard_map/ppermute | solution.py:18
  67.7 21.2 %collective-permute-start.2 = (bf16[2,2,128,128]{2,3,0,1:T(8,128)(2,1)S(1)}, bf16[2,2,128,128]{2,3,0,1:T(8,128)(2,1)S(1)}, u32[]{:S(2)}, u32[]{:S(2)}) collective-permute-start(bf16[2,2,128,128]{2,3,0,1:T(8,128)(2,1)S(1)} %pad_maximum_fusion.1), channel_id=1, source_target_pairs={{0,1},{1,2},{2,3},{3,4},{4,5},{5,6},{6,7},{7,8},{8,9},{9,10},{10,1... | collective-permute-start | bytes 393224 | tf_op jit(solution)/shard_map/ppermute | solution.py:15
  70.3 8.1 %collective-permute-start.15 = (bf16[2,2,128,128]{3,2,0,1:T(8,128)(2,1)S(1)}, bf16[2,2,128,128]{3,2,0,1:T(8,128)(2,1)S(1)}, u32[]{:S(2)}, u32[]{:S(2)}) collective-permute-start(bf16[2,2,128,128]{3,2,0,1:T(8,128)(2,1)S(1)} %broadcast_select_fusion), channel_id=1, source_target_pairs={{64,0},{96,32},{128,64},{160,96},{192,128},{224,160},{256,192},{28... | collective-permute-start | bytes 393224 | tf_op jit(solution)/shard_map/ppermute | solution.py:26
  78.5 12.5 %collective-permute-start.16 = (bf16[2,2,128,128]{3,2,0,1:T(8,128)(2,1)S(1)}, bf16[2,2,128,128]{3,2,0,1:T(8,128)(2,1)S(1)}, u32[]{:S(2)}, u32[]{:S(2)}) collective-permute-start(bf16[2,2,128,128]{3,2,0,1:T(8,128)(2,1)S(1)} %broadcast_select_fusion.2), channel_id=1, source_target_pairs={{128,0},{160,32},{192,64},{224,96},{256,128},{288,160},{320,192},{... | collective-permute-start | bytes 393224 | tf_op jit(solution)/shard_map/ppermute | solution.py:26
  91.1 20.6 %collective-permute-start.17 = (bf16[2,2,128,128]{3,2,0,1:T(8,128)(2,1)S(1)}, bf16[2,2,128,128]{3,2,0,1:T(8,128)(2,1)S(1)}, u32[]{:S(2)}, u32[]{:S(2)}) collective-permute-start(bf16[2,2,128,128]{3,2,0,1:T(8,128)(2,1)S(1)} %broadcast_select_fusion.4), channel_id=1, source_target_pairs={{1,0},{2,1},{3,2},{4,3},{5,4},{6,5},{7,6},{8,7},{9,8},{10,9},{11,1... | collective-permute-start | bytes 393224 | tf_op jit(solution)/shard_map/ppermute | solution.py:26
  111.8 8.7 %collective-permute-start.18 = (bf16[2,2,128,128]{3,2,0,1:T(8,128)(2,1)S(1)}, bf16[2,2,128,128]{3,2,0,1:T(8,128)(2,1)S(1)}, u32[]{:S(2)}, u32[]{:S(2)}) collective-permute-start(bf16[2,2,128,128]{3,2,0,1:T(8,128)(2,1)S(1)} %broadcast_select_fusion.6), channel_id=1, source_target_pairs={{2,0},{3,1},{4,2},{5,3},{6,4},{7,5},{8,6},{9,7},{10,8},{11,9},{12,... | collective-permute-start | bytes 393224 | tf_op jit(solution)/shard_map/ppermute | solution.py:26
  120.5 12.8 %collective-permute-start.19 = (bf16[2,2,128,128]{3,2,0,1:T(8,128)(2,1)S(1)}, bf16[2,2,128,128]{3,2,0,1:T(8,128)(2,1)S(1)}, u32[]{:S(2)}, u32[]{:S(2)}) collective-permute-start(bf16[2,2,128,128]{3,2,0,1:T(8,128)(2,1)S(1)} %broadcast_select_fusion.8), channel_id=1, source_target_pairs={{4,0},{5,1},{6,2},{7,3},{8,4},{9,5},{10,6},{11,7},{12,8},{13,9},{1... | collective-permute-start | bytes 393224 | tf_op jit(solution)/shard_map/ppermute | solution.py:26
  133.4 24.5 %collective-permute-start.21 = (bf16[2,2,128,128]{3,2,0,1:T(8,128)(2,1)S(1)}, bf16[2,2,128,128]{3,2,0,1:T(8,128)(2,1)S(1)}, u32[]{:S(2)}, u32[]{:S(2)}) collective-permute-start(bf16[2,2,128,128]{3,2,0,1:T(8,128)(2,1)S(1)} %broadcast_select_fusion.10), channel_id=1, source_target_pairs={{0,1},{1,2},{2,3},{3,4},{4,5},{5,6},{6,7},{7,8},{8,9},{9,10},{10,1... | collective-permute-start | bytes 393224 | tf_op jit(solution)/shard_map/ppermute | solution.py:15
  144.0 15.4 %collective-permute-start.20 = (bf16[2,2,128,128]{3,2,0,1:T(8,128)(2,1)S(1)}, bf16[2,2,128,128]{3,2,0,1:T(8,128)(2,1)S(1)}, u32[]{:S(2)}, u32[]{:S(2)}) collective-permute-start(bf16[2,2,128,128]{3,2,0,1:T(8,128)(2,1)S(1)} %broadcast_select_fusion.10), channel_id=1, source_target_pairs={{1,0},{2,1},{3,2},{4,3},{5,4},{6,5},{7,6},{8,7},{9,8},{10,9},{11,1... | collective-permute-start | bytes 393224 | tf_op jit(solution)/shard_map/ppermute | solution.py:18
  160.9 6.3 %collective-permute-start.23 = (bf16[2,2,128,128]{3,2,0,1:T(8,128)(2,1)S(1)}, bf16[2,2,128,128]{3,2,0,1:T(8,128)(2,1)S(1)}, u32[]{:S(2)}, u32[]{:S(2)}) collective-permute-start(bf16[2,2,128,128]{3,2,0,1:T(8,128)(2,1)S(1)} %pad_maximum_fusion.5), channel_id=1, source_target_pairs={{0,32},{32,64},{64,96},{96,128},{128,160},{160,192},{192,224},{224... | collective-permute-start | bytes 393224 | tf_op jit(solution)/shard_map/ppermute | solution.py:15
  162.9 6.1 %collective-permute-start.22 = (bf16[2,2,128,128]{3,2,0,1:T(8,128)(2,1)S(1)}, bf16[2,2,128,128]{3,2,0,1:T(8,128)(2,1)S(1)}, u32[]{:S(2)}, u32[]{:S(2)}) collective-permute-start(bf16[2,2,128,128]{3,2,0,1:T(8,128)(2,1)S(1)} %pad_maximum_fusion.5), channel_id=1, source_target_pairs={{32,0},{64,32},{96,64},{128,96},{160,128},{192,160},{224,192},{256... | collective-permute-start | bytes 393224 | tf_op jit(solution)/shard_map/ppermute | solution.py:18
  170.6 20.2 %collective-permute-start.25 = (bf16[2,2,128,128]{3,2,0,1:T(8,128)(2,1)S(1)}, bf16[2,2,128,128]{3,2,0,1:T(8,128)(2,1)S(1)}, u32[]{:S(2)}, u32[]{:S(2)}) collective-permute-start(bf16[2,2,128,128]{3,2,0,1:T(8,128)(2,1)S(1)} %pad_maximum_fusion.6), channel_id=1, source_target_pairs={{0,1},{1,2},{2,3},{3,4},{4,5},{5,6},{6,7},{7,8},{8,9},{9,10},{10,1... | collective-permute-start | bytes 393224 | tf_op jit(solution)/shard_map/ppermute | solution.py:15
  172.5 21.6 %collective-permute-start.24 = (bf16[2,2,128,128]{3,2,0,1:T(8,128)(2,1)S(1)}, bf16[2,2,128,128]{3,2,0,1:T(8,128)(2,1)S(1)}, u32[]{:S(2)}, u32[]{:S(2)}) collective-permute-start(bf16[2,2,128,128]{3,2,0,1:T(8,128)(2,1)S(1)} %pad_maximum_fusion.6), channel_id=1, source_target_pairs={{1,0},{2,1},{3,2},{4,3},{5,4},{6,5},{7,6},{8,7},{9,8},{10,9},{11,1... | collective-permute-start | bytes 393224 | tf_op jit(solution)/shard_map/ppermute | solution.py:18
  183.3 18.2 %collective-permute-start.5 = (bf16[2,2,128,128]{3,2,0,1:T(8,128)(2,1)S(1)}, bf16[2,2,128,128]{3,2,0,1:T(8,128)(2,1)S(1)}, u32[]{:S(2)}, u32[]{:S(2)}) collective-permute-start(bf16[2,2,128,128]{3,2,0,1:T(8,128)(2,1)S(1)} %pad_maximum_fusion.2), channel_id=1, source_target_pairs={{32,0},{64,32},{96,64},{128,96},{160,128},{192,160},{224,192},{256... | collective-permute-start | bytes 393224 | tf_op jit(solution)/shard_map/ppermute | solution.py:18
  187.1 15.0 %collective-permute-start.4 = (bf16[2,2,128,128]{3,2,0,1:T(8,128)(2,1)S(1)}, bf16[2,2,128,128]{3,2,0,1:T(8,128)(2,1)S(1)}, u32[]{:S(2)}, u32[]{:S(2)}) collective-permute-start(bf16[2,2,128,128]{3,2,0,1:T(8,128)(2,1)S(1)} %pad_maximum_fusion.2), channel_id=1, source_target_pairs={{0,32},{32,64},{64,96},{96,128},{128,160},{160,192},{192,224},{224... | collective-permute-start | bytes 393224 | tf_op jit(solution)/shard_map/ppermute | solution.py:15
  195.3 37.1 %collective-permute-start.27 = (bf16[2,2,128,128]{3,2,0,1:T(8,128)(2,1)S(1)}, bf16[2,2,128,128]{3,2,0,1:T(8,128)(2,1)S(1)}, u32[]{:S(2)}, u32[]{:S(2)}) collective-permute-start(bf16[2,2,128,128]{3,2,0,1:T(8,128)(2,1)S(1)} %pad_maximum_fusion.7), channel_id=1, source_target_pairs={{0,32},{32,64},{64,96},{96,128},{128,160},{160,192},{192,224},{224... | collective-permute-start | bytes 393224 | tf_op jit(solution)/shard_map/ppermute | solution.py:15
  197.5 35.3 %collective-permute-start.26 = (bf16[2,2,128,128]{3,2,0,1:T(8,128)(2,1)S(1)}, bf16[2,2,128,128]{3,2,0,1:T(8,128)(2,1)S(1)}, u32[]{:S(2)}, u32[]{:S(2)}) collective-permute-start(bf16[2,2,128,128]{3,2,0,1:T(8,128)(2,1)S(1)} %pad_maximum_fusion.7), channel_id=1, source_target_pairs={{32,0},{64,32},{96,64},{128,96},{160,128},{192,160},{224,192},{256... | collective-permute-start | bytes 393224 | tf_op jit(solution)/shard_map/ppermute | solution.py:18
  203.5 15.8 %collective-permute-start.7 = (bf16[2,2,128,128]{2,3,0,1:T(8,128)(2,1)S(1)}, bf16[2,2,128,128]{2,3,0,1:T(8,128)(2,1)S(1)}, u32[]{:S(2)}, u32[]{:S(2)}) collective-permute-start(bf16[2,2,128,128]{2,3,0,1:T(8,128)(2,1)S(1)} %pad_maximum_fusion.3), channel_id=1, source_target_pairs={{1,0},{2,1},{3,2},{4,3},{5,4},{6,5},{7,6},{8,7},{9,8},{10,9},{11,1... | collective-permute-start | bytes 393224 | tf_op jit(solution)/shard_map/ppermute | solution.py:18
  213.9 15.3 %collective-permute-start.6 = (bf16[2,2,128,128]{2,3,0,1:T(8,128)(2,1)S(1)}, bf16[2,2,128,128]{2,3,0,1:T(8,128)(2,1)S(1)}, u32[]{:S(2)}, u32[]{:S(2)}) collective-permute-start(bf16[2,2,128,128]{2,3,0,1:T(8,128)(2,1)S(1)} %pad_maximum_fusion.3), channel_id=1, source_target_pairs={{0,1},{1,2},{2,3},{3,4},{4,5},{5,6},{6,7},{7,8},{8,9},{9,10},{10,1... | collective-permute-start | bytes 393224 | tf_op jit(solution)/shard_map/ppermute | solution.py:15
  230.5 6.3 %collective-permute-start.8 = (bf16[2,2,128,128]{3,2,0,1:T(8,128)(2,1)S(1)}, bf16[2,2,128,128]{3,2,0,1:T(8,128)(2,1)S(1)}, u32[]{:S(2)}, u32[]{:S(2)}) collective-permute-start(bf16[2,2,128,128]{3,2,0,1:T(8,128)(2,1)S(1)} %pad_maximum_fusion.4), channel_id=1, source_target_pairs={{992,0},{0,32},{32,64},{64,96},{96,128},{128,160},{160,192},{192,2... | collective-permute-start | bytes 393224 | tf_op jit(solution)/shard_map/ppermute | solution.py:26
  236.8 8.8 %collective-permute-start.9 = (bf16[2,2,128,128]{3,2,0,1:T(8,128)(2,1)S(1)}, bf16[2,2,128,128]{3,2,0,1:T(8,128)(2,1)S(1)}, u32[]{:S(2)}, u32[]{:S(2)}) collective-permute-start(bf16[2,2,128,128]{3,2,0,1:T(8,128)(2,1)S(1)} %broadcast_select_fusion.1), channel_id=1, source_target_pairs={{960,0},{992,32},{0,64},{32,96},{64,128},{96,160},{128,192},{160,2... | collective-permute-start | bytes 393224 | tf_op jit(solution)/shard_map/ppermute | solution.py:26
  245.8 21.4 %collective-permute-start.10 = (bf16[2,2,128,128]{3,2,0,1:T(8,128)(2,1)S(1)}, bf16[2,2,128,128]{3,2,0,1:T(8,128)(2,1)S(1)}, u32[]{:S(2)}, u32[]{:S(2)}) collective-permute-start(bf16[2,2,128,128]{3,2,0,1:T(8,128)(2,1)S(1)} %broadcast_select_fusion.3), channel_id=1, source_target_pairs={{896,0},{928,32},{960,64},{992,96},{0,128},{32,160},{64,192},{96,2... | collective-permute-start | bytes 393224 | tf_op jit(solution)/shard_map/ppermute | solution.py:26
  267.3 20.7 %collective-permute-start.11 = (bf16[2,2,128,128]{3,2,0,1:T(8,128)(2,1)S(1)}, bf16[2,2,128,128]{3,2,0,1:T(8,128)(2,1)S(1)}, u32[]{:S(2)}, u32[]{:S(2)}) collective-permute-start(bf16[2,2,128,128]{3,2,0,1:T(8,128)(2,1)S(1)} %broadcast_select_fusion.5), channel_id=1, source_target_pairs={{31,0},{0,1},{1,2},{2,3},{3,4},{4,5},{5,6},{6,7},{7,8},{8,9},{9,10... | collective-permute-start | bytes 393224 | tf_op jit(solution)/shard_map/ppermute | solution.py:26
  288.1 13.8 %collective-permute-start.12 = (bf16[2,2,128,128]{3,2,0,1:T(8,128)(2,1)S(1)}, bf16[2,2,128,128]{3,2,0,1:T(8,128)(2,1)S(1)}, u32[]{:S(2)}, u32[]{:S(2)}) collective-permute-start(bf16[2,2,128,128]{3,2,0,1:T(8,128)(2,1)S(1)} %broadcast_select_fusion.7), channel_id=1, source_target_pairs={{30,0},{31,1},{0,2},{1,3},{2,4},{3,5},{4,6},{5,7},{6,8},{7,9},{8,1... | collective-permute-start | bytes 393224 | tf_op jit(solution)/shard_map/ppermute | solution.py:26
  301.9 15.6 %collective-permute-start.13 = (bf16[2,2,128,128]{3,2,0,1:T(8,128)(2,1)S(1)}, bf16[2,2,128,128]{3,2,0,1:T(8,128)(2,1)S(1)}, u32[]{:S(2)}, u32[]{:S(2)}) collective-permute-start(bf16[2,2,128,128]{3,2,0,1:T(8,128)(2,1)S(1)} %broadcast_select_fusion.9), channel_id=1, source_target_pairs={{28,0},{29,1},{30,2},{31,3},{0,4},{1,5},{2,6},{3,7},{4,8},{5,9},{6... | collective-permute-start | bytes 393224 | tf_op jit(solution)/shard_map/ppermute | solution.py:26
where the time goes:
time: 320 us; the launch traced here: 318 us
  starting transfers between devices  142 us (44%)
  waiting for transfers between devices  117 us (37%)
  between operations  28.5 us (9%)
  matrix products  18.1 us (6%)
  local copies, waits for them, and re-layouts  6.75 us (2%)
  other arithmetic  6.56 us (2%)
    ppermute x12, waiting for transfers between devices, from_behind(): return lax.ppermute(block, axis, route)  98.6 us
    ppermute x8, starting transfers between devices, with_halo(): lax.ppermute(lax.slice_in_dim(block, 0, width, axis=dim), axis, backward)  68.1 us
    ppermute x12, starting transfers between devices, from_behind(): return lax.ppermute(block, axis, route)  48.9 us
    ppermute x8, starting transfers between devices, with_halo(): lax.ppermute(lax.slice_in_dim(block, block.shape[dim] - width, None, axis...  24.7 us
    ppermute x8, waiting for transfers between devices, with_halo(): lax.ppermute(lax.slice_in_dim(block, block.shape[dim] - width, None, axis...  10.1 us
    dot_general x48, matrix products, rows_product(): jnp.einsum(form, matrix, blocks, preferred_element_type=jnp.float32)  9.39 us
    dot_general x48, matrix products, cols_product(): jnp.einsum(form, blocks, matrix, preferred_element_type=jnp.float32)  8.68 us
    ppermute x8, waiting for transfers between devices, with_halo(): lax.ppermute(lax.slice_in_dim(block, 0, width, axis=dim), axis, backward)  7.98 us
  transfers between devices with their start and end apart: 28, of which 18 were waited for; matrix products, arithmetic and copies ran while one was open for 6% of the time, Pallas kernels for 0%

commit v1 on v0

v1 whole, which is shorter than its diff:
```python
import functools
import math

import jax
import jax.numpy as jnp
from jax import lax
from jax.experimental import pallas as pl
from jax.experimental.pallas import tpu as pltpu
from jax.sharding import PartitionSpec as P

MESH = pl.DeviceIdType.MESH
SHIFTS = 8


def left_matrix(bank, index):
    real, imag = bank[index, 0], bank[index, 1]
    return jnp.concatenate(
        [jnp.concatenate([real, -imag], axis=1), jnp.concatenate([imag, real], axis=1)], axis=0
    )


def left_adjoint(bank, index):
    real = bank[index, 0].astype(jnp.float32).T.astype(jnp.bfloat16)
    imag = bank[index, 1].astype(jnp.float32).T.astype(jnp.bfloat16)
    return jnp.concatenate(
        [jnp.concatenate([real, imag], axis=1), jnp.concatenate([-imag, real], axis=1)], axis=0
    )


def right_matrix(bank, index):
    real, imag = bank[index, 0], bank[index, 1]
    return jnp.concatenate(
        [jnp.concatenate([real, imag], axis=1), jnp.concatenate([-imag, real], axis=1)], axis=0
    )


def by_component(ref):
    return jnp.concatenate(
        [
            jnp.concatenate([ref[0, 0], ref[1, 0]], axis=1),
            jnp.concatenate([ref[0, 1], ref[1, 1]], axis=1),
        ],
        axis=0,
    )


def by_angle(ref):
    return jnp.concatenate(
        [
            jnp.concatenate([ref[0, 0], ref[0, 1]], axis=1),
            jnp.concatenate([ref[1, 0], ref[1, 1]], axis=1),
        ],
        axis=0,
    )


def row_term(matrix, ref):
    return jnp.dot(matrix, by_component(ref), preferred_element_type=jnp.float32)


def col_term(ref, matrix):
    return jnp.dot(by_angle(ref), matrix, preferred_element_type=jnp.float32)


def col_adjoint_term(ref, matrix):
    return lax.dot_general(
        by_angle(ref), matrix, (((1,), (1,)), ((), ())), preferred_element_type=jnp.float32
    )


def from_component(total, angle, part):
    n = total.shape[0] // 2
    return total[part * n : (part + 1) * n, angle * n : (angle + 1) * n]


def from_angle(total, angle, part):
    n = total.shape[0] // 2
    return total[angle * n : (angle + 1) * n, part * n : (part + 1) * n]


def incident(tilt, row_start, col_start, period, width):
    line = lax.broadcasted_iota(jnp.int32, (8, width), 0)
    spot = lax.broadcasted_iota(jnp.int32, (8, width), 1)
    rate = jnp.where(
        line == 0,
        tilt[0, 0],
        jnp.where(line == 1, tilt[0, 1], jnp.where(line == 2, tilt[1, 0], tilt[1, 1])),
    )
    start = jnp.where(line % 2 == 0, row_start, col_start)
    turns = (rate * (start + spot)) & (period - 1)
    phase = turns.astype(jnp.float32) * (2.0 * math.pi / period)
    cos, sin = jnp.cos(phase), jnp.sin(phase)
    cos_t, sin_t = cos.T, sin.T
    fields = []
    for angle in range(2):
        row_cos = cos_t[:, 2 * angle : 2 * angle + 1]
        row_sin = sin_t[:, 2 * angle : 2 * angle + 1]
        col_cos = cos[2 * angle + 1 : 2 * angle + 2, :]
        col_sin = sin[2 * angle + 1 : 2 * angle + 2, :]
        fields.append(
            (
                (row_cos * col_cos - row_sin * col_sin).astype(jnp.bfloat16),
                (row_sin * col_cos + row_cos * col_sin).astype(jnp.bfloat16),
            )
        )
    return fields


class Halo:
    def __init__(self, axis, count, source, low, high, sems, slot):
        here = lax.axis_index(axis)
        after = lax.rem(here + 1, count)
        before = lax.rem(here + count - 1, count)
        send, recv = sems
        self.up = pltpu.make_async_remote_copy(
            src_ref=source,
            dst_ref=low,
            send_sem=send.at[slot],
            recv_sem=recv.at[slot],
            device_id={axis: after},
            device_id_type=MESH,
        )
        self.down = pltpu.make_async_remote_copy(
            src_ref=source,
            dst_ref=high,
            send_sem=send.at[slot + 1],
            recv_sem=recv.at[slot + 1],
            device_id={axis: before},
            device_id_type=MESH,
        )

    def start(self):
        self.up.start()
        self.down.start()

    def wait_send(self):
        self.up.wait_send()
        self.down.wait_send()


def greet(axes):
    barrier = pltpu.get_barrier_semaphore()
    for axis, count in axes:
        here = lax.axis_index(axis)
        for other in (lax.rem(here + 1, count), lax.rem(here + count - 1, count)):
            pl.semaphore_signal(barrier, inc=1, device_id={axis: other}, device_id_type=MESH)


def met(number):
    pl.semaphore_wait(pltpu.get_barrier_semaphore(), number)


def first(rows, cols, order, band, tilt, obj, bank, cot, u_out, psi_out, q_out, *scratch):
    u_mine, v_mine, h_mine, rim, send, recv = scratch
    width = bank.shape[2]
    greet((("row", rows), ("col", cols)))
    row_start = lax.axis_index("row") * width
    col_start = lax.axis_index("col") * width
    here, later = order[0], order[1]
    fields = incident(tilt, row_start, col_start, rows * width, width)
    t_real, t_imag = obj[here, 0], obj[here, 1]
    for angle in range(2):
        real = fields[angle][0].astype(jnp.float32)
        imag = fields[angle][1].astype(jnp.float32)
        u_mine[angle, 0] = (t_real * real - t_imag * imag).astype(jnp.bfloat16)
        u_mine[angle, 1] = (t_real * imag + t_imag * real).astype(jnp.bfloat16)
    met(4)
    sems = (send, recv)
    halo_u = Halo("row", rows, u_mine, rim.at[0], rim.at[1], sems, 0)
    halo_g = Halo("col", cols, cot, rim.at[2], rim.at[3], sems, 2)
    halo_v = Halo("col", cols, v_mine, rim.at[4], rim.at[5], sems, 4)
    halo_h = Halo("row", rows, h_mine, rim.at[6], rim.at[7], sems, 6)
    halo_g.start()
    halo_u.start()
    v = row_term(left_matrix(bank, band[0, 0, 1]), u_mine)
    h = col_adjoint_term(cot, right_matrix(bank, band[1, 1, 1]))
    halo_u.up.wait_recv()
    v += row_term(left_matrix(bank, band[0, 0, 0]), rim.at[0])
    halo_u.down.wait_recv()
    v += row_term(left_matrix(bank, band[0, 0, 2]), rim.at[1])
    for angle in range(2):
        for part in range(2):
            v_mine[angle, part] = from_component(v, angle, part).astype(jnp.bfloat16)
    halo_v.start()
    halo_g.up.wait_recv()
    h += col_adjoint_term(rim.at[2], right_matrix(bank, band[1, 1, 2]))
    halo_g.down.wait_recv()
    h += col_adjoint_term(rim.at[3], right_matrix(bank, band[1, 1, 0]))
    for angle in range(2):
        for part in range(2):
            h_mine[angle, part] = from_angle(h, angle, part).astype(jnp.bfloat16)
    halo_h.start()
    q = row_term(left_adjoint(bank, band[1, 0, 1]), h_mine)
    p = col_term(v_mine, right_matrix(bank, band[0, 1, 1]))
    halo_h.up.wait_recv()
    q += row_term(left_adjoint(bank, band[1, 0, 2]), rim.at[6])
    halo_h.down.wait_recv()
    q += row_term(left_adjoint(bank, band[1, 0, 0]), rim.at[7])
    for angle in range(2):
        for part in range(2):
            q_out[angle, part] = from_component(q, angle, part).astype(jnp.bfloat16)
    halo_v.up.wait_recv()
    p += col_term(rim.at[4], right_matrix(bank, band[0, 1, 0]))
    halo_v.down.wait_recv()
    p += col_term(rim.at[5], right_matrix(bank, band[0, 1, 2]))
    s_real, s_imag = obj[later, 0], obj[later, 1]
    for angle in range(2):
        real = from_angle(p, angle, 0).astype(jnp.bfloat16)
        imag = from_angle(p, angle, 1).astype(jnp.bfloat16)
        psi_out[angle, 0] = real
        psi_out[angle, 1] = imag
        real, imag = real.astype(jnp.float32), imag.astype(jnp.float32)
        u_out[angle, 0] = (s_real * real - s_imag * imag).astype(jnp.bfloat16)
        u_out[angle, 1] = (s_real * imag + s_imag * real).astype(jnp.bfloat16)
    for halo in (halo_u, halo_g, halo_v, halo_h):
        halo.wait_send()


def second(rows, cols, order, band, tilt, obj, bank, u, q, psi, exit_out, grad_out, *scratch):
    g_mine, v_mine, h_mine, rim, send, recv = scratch
    width = bank.shape[2]
    greet((("row", rows), ("col", cols)))
    row_start = lax.axis_index("row") * width
    col_start = lax.axis_index("col") * width
    later = order[1]
    s_real, s_imag = obj[later, 0], obj[later, 1]
    last_real = None
    last_imag = None
    for angle in range(2):
        q_real, q_imag = q[angle, 0].astype(jnp.float32), q[angle, 1].astype(jnp.float32)
        g_mine[angle, 0] = (q_real * s_real + q_imag * s_imag).astype(jnp.bfloat16)
        g_mine[angle, 1] = (q_imag * s_real - q_real * s_imag).astype(jnp.bfloat16)
        real, imag = psi[angle, 0].astype(jnp.float32), psi[angle, 1].astype(jnp.float32)
        add_real = q_real * real + q_imag * imag
        add_imag = q_imag * real - q_real * imag
        last_real = add_real if last_real is None else last_real + add_real
        last_imag = add_imag if last_imag is None else last_imag + add_imag
    met(4)
    sems = (send, recv)
    halo_u = Halo("row", rows, u, rim.at[0], rim.at[1], sems, 0)
    halo_g = Halo("col", cols, g_mine, rim.at[2], rim.at[3], sems, 2)
    halo_v = Halo("col", cols, v_mine, rim.at[4], rim.at[5], sems, 4)
    halo_h = Halo("row", rows, h_mine, rim.at[6], rim.at[7], sems, 6)
    halo_g.start()
    halo_u.start()
    v = row_term(left_matrix(bank, band[1, 0, 1]), u)
    h = col_adjoint_term(g_mine, right_matrix(bank, band[0, 1, 1]))
    halo_u.up.wait_recv()
    v += row_term(left_matrix(bank, band[1, 0, 0]), rim.at[0])
    halo_u.down.wait_recv()
    v += row_term(left_matrix(bank, band[1, 0, 2]), rim.at[1])
    for angle in range(2):
        for part in range(2):
            v_mine[angle, part] = from_component(v, angle, part).astype(jnp.bfloat16)
    halo_v.start()
    halo_g.up.wait_recv()
    h += col_adjoint_term(rim.at[2], right_matrix(bank, band[0, 1, 2]))
    halo_g.down.wait_recv()
    h += col_adjoint_term(rim.at[3], right_matrix(bank, band[0, 1, 0]))
    for angle in range(2):
        for part in range(2):
            h_mine[angle, part] = from_angle(h, angle, part).astype(jnp.bfloat16)
    halo_h.start()
    fields = incident(tilt, row_start, col_start, rows * width, width)
    b = row_term(left_adjoint(bank, band[0, 0, 1]), h_mine)
    p = col_term(v_mine, right_matrix(bank, band[1, 1, 1]))
    halo_h.up.wait_recv()
    b += row_term(left_adjoint(bank, band[0, 0, 2]), rim.at[6])
    halo_h.down.wait_recv()
    b += row_term(left_adjoint(bank, band[0, 0, 0]), rim.at[7])
    first_real = None
    first_imag = None
    for angle in range(2):
        q_real = from_component(b, angle, 0).astype(jnp.bfloat16).astype(jnp.float32)
        q_imag = from_component(b, angle, 1).astype(jnp.bfloat16).astype(jnp.float32)
        real, imag = fields[angle][0].astype(jnp.float32), fields[angle][1].astype(jnp.float32)
        add_real = q_real * real + q_imag * imag
        add_imag = q_imag * real - q_real * imag
        first_real = add_real if first_real is None else first_real + add_real
        first_imag = add_imag if first_imag is None else first_imag + add_imag
    swapped = later == 0
    grad_out[0, 0] = jnp.where(swapped, last_real, first_real)
    grad_out[0, 1] = jnp.where(swapped, last_imag, first_imag)
    grad_out[1, 0] = jnp.where(swapped, first_real, last_real)
    grad_out[1, 1] = jnp.where(swapped, first_imag, last_imag)
    halo_v.up.wait_recv()
    p += col_term(rim.at[4], right_matrix(bank, band[1, 1, 0]))
    halo_v.down.wait_recv()
    p += col_term(rim.at[5], right_matrix(bank, band[1, 1, 2]))
    for angle in range(2):
        for part in range(2):
            exit_out[angle, part] = from_angle(p, angle, part).astype(jnp.bfloat16)
    for halo in (halo_u, halo_g, halo_v, halo_h):
        halo.wait_send()


def call(body, outs, arrays, width, number):
    field = (2, 2, width, width)
    smem = pl.BlockSpec(memory_space=pltpu.SMEM)
    vmem = pl.BlockSpec(memory_space=pltpu.VMEM)
    return pl.pallas_call(
        body,
        out_shape=outs,
        in_specs=[smem] * 3 + [vmem] * (len(arrays) - 3),
        out_specs=[vmem] * len(outs),
        scratch_shapes=[
            pltpu.VMEM(field, jnp.bfloat16),
            pltpu.VMEM(field, jnp.bfloat16),
            pltpu.VMEM(field, jnp.bfloat16),
            pltpu.VMEM((8, *field), jnp.bfloat16),
            pltpu.SemaphoreType.DMA((8,)),
            pltpu.SemaphoreType.DMA((8,)),
        ],
        compiler_params=pltpu.CompilerParams(collective_id=number, has_side_effects=True),
    )(*arrays)


def move(row_step, col_step, rows, cols, u, q):
    if row_step == 0 and col_step == 0:
        return u, q
    there = []
    for row in range(rows):
        for col in range(cols):
            target = (row + row_step) % rows * cols + (col + col_step) % cols
            there.append((row * cols + col, target))
    back = [(target, source) for source, target in there]
    axes = ("row", "col")
    return lax.ppermute(u, axes, there), lax.ppermute(q, axes, back)


def local(rows, cols, obj, bank, band_index, tilt, tile_shift, slice_order, cot):
    width = bank.shape[2]
    small = jax.ShapeDtypeStruct(cot.shape, jnp.bfloat16)
    u, psi, q = call(
        functools.partial(first, rows, cols),
        (small, small, small),
        (slice_order, band_index, tilt, obj, bank, cot),
        width,
        0,
    )
    choice = tile_shift[:, 0] * SHIFTS + tile_shift[:, 1]
    branches = [
        functools.partial(move, row_step, col_step, rows, cols)
        for row_step in range(SHIFTS)
        for col_step in range(SHIFTS)
    ]
    moved = [lax.switch(choice[angle], branches, u[angle], q[angle]) for angle in range(2)]
    u = jnp.stack([moved[0][0], moved[1][0]])
    q = jnp.stack([moved[0][1], moved[1][1]])
    exit_field, grad = call(
        functools.partial(second, rows, cols),
        (small, jax.ShapeDtypeStruct(obj.shape, jnp.float32)),
        (slice_order, band_index, tilt, obj, bank, u, q, psi),
        width,
        1,
    )
    return exit_field, grad


def solution(mesh):
    field = P(None, None, "row", "col")
    return jax.shard_map(
        functools.partial(local, mesh.shape["row"], mesh.shape["col"]),
        mesh=mesh,
        in_specs=(field, P(), P(), P(), P(), P(), field),
        out_specs=(field, field),
        check_vma=False,
    )
```

time: 320 us -> 208 us (0.65)
  the two profiles are of different devices: /device:TPU:4 before, /device:TPU:71 now
where the time goes in v1:
time: 208 us
  Pallas kernels  135 us (65%)
  starting transfers between devices  53.4 us (26%)
  waiting for transfers between devices  11.1 us (5%)
  local copies, waits for them, and re-layouts  3.81 us (2%)
  other arithmetic  2.16 us (1%)
    pallas_call x2, Pallas kernels, call(): pl.pallas_call(body, out_shape=outs, in_specs=[smem] * 3 + [vmem] * (len(...  135 us
    ppermute x4, starting transfers between devices, move(): return (lax.ppermute(u, axes, there), lax.ppermute(q, axes, back))  53.4 us
    ppermute x4, waiting for transfers between devices, move(): return (lax.ppermute(u, axes, there), lax.ppermute(q, axes, back))  11.1 us
  transfers between devices with their start and end apart: 4, of which 3 were waited for; matrix products, arithmetic and copies ran while one was open for 0% of the time, Pallas kernels for 0%

profile of v1, /device:TPU:71, one launch (start us, length us, event | category | flops | bytes accessed | tf_op | source)
XLA Modules:
  0.0 207.5 jit_solution(4792984023591507761)
XLA Ops:
  0.6 0.8 slice_add_fusion
  1.5 0.5 fusion
  3.3 69.3 %shard_map.86 = (bf16[2,2,128,128]{3,2,1,0:T(8,128)(2,1)}, bf16[2,2,128,128]{3,2,1,0:T(8,128)(2,1)}, bf16[2,2,128,128]{3,2,1,0:T(8,128)(2,1)}) custom-call(s32[2]{0:T(128)} %order.3, s32[2,2,3]{2,1,0:T(2,128)} %band.3, s32[2,2]{1,0:T(2,128)} %tilt.3, f32[2,2,128,128]{3,2,1,0:T(8,128)} %obj.3, bf16[8,2,128,128]{3,2,1,0:T(8,128)(2,1)} %bank.3, ...), custom_call_target="tpu_custom_call" | custom-call | tf_op jit(solution)/shard_map/pallas_call | solution.py:301
  72.6 1.0 slice_bitcast_fusion.2
  73.6 44.4 %conditional.2 = ((bf16[2,128,128]{2,1,0:T(8,128)(2,1)S(1)}, bf16[2,128,128]{2,1,0:T(8,128)(2,1)S(1)})) conditional(s32[]{:T(128)} %bitcast, (bf16[2,128,128]{2,1,0:T(8,128)(2,1)S(1)}, bf16[2,128,128]{2,1,0:T(8,128)(2,1)S(1)}) %tuple.1289, (bf16[2,128,128]{2,1,0:T(8,128)(2,1)S(1)}, ...), branch_computations={%region_0.0_spmd, %region_1.0_spmd, %region_2.0_spmd, %region_3.0_... | conditional | bytes 786536 | solution.py:347
  73.6 14.6 %collective-permute-start.114 = (bf16[2,128,128]{2,1,0:T(8,128)(2,1)S(1)}, bf16[2,128,128]{2,1,0:T(8,128)(2,1)S(1)}, u32[]{:S(2)}, u32[]{:S(2)}) collective-permute-start(bf16[2,128,128]{2,1,0:T(8,128)(2,1)S(1)} %get-tuple-element.650), channel_id=1, source_target_pairs={{0,226},{1,227},{2,228},{3,229},{4,230},{5,231},{6,232},{7,233},{8... | collective-permute-start | bytes 196616 | tf_op jit(solution)/shard_map/cond/branch_58_fun/ppermute | solution.py:328
  88.2 23.7 %collective-permute-start.115 = (bf16[2,128,128]{2,1,0:T(8,128)(2,1)S(1)}, bf16[2,128,128]{2,1,0:T(8,128)(2,1)S(1)}, u32[]{:S(2)}, u32[]{:S(2)}) collective-permute-start(bf16[2,128,128]{2,1,0:T(8,128)(2,1)S(1)} %get-tuple-element.651), channel_id=1, source_target_pairs={{226,0},{227,1},{228,2},{229,3},{230,4},{231,5},{232,6},{233,7},{2... | collective-permute-start | bytes 196616 | tf_op jit(solution)/shard_map/cond/branch_58_fun/ppermute | solution.py:328
  111.9 0.0 collective-permute-done.114
  111.9 6.1 %collective-permute-done.115 = bf16[2,128,128]{2,1,0:T(8,128)(2,1)S(1)} collective-permute-done((bf16[2,128,128]{2,1,0:T(8,128)(2,1)S(1)}, bf16[2,128,128]{2,1,0:T(8,128)(2,1)S(1)}, u32[]{:S(2)}, u32[]{:S(2)}) %collective-permute-start.115) | collective-permute-done | bytes 65568 | tf_op jit(solution)/shard_map/cond/branch_58_fun/ppermute | solution.py:328
  118.0 20.2 %conditional.3 = ((bf16[2,128,128]{2,1,0:T(8,128)(2,1)S(1)}, bf16[2,128,128]{2,1,0:T(8,128)(2,1)S(1)})) conditional(s32[]{:T(128)} %bitcast.4, (bf16[2,128,128]{2,1,0:T(8,128)(2,1)S(1)}, bf16[2,128,128]{2,1,0:T(8,128)(2,1)S(1)}) %tuple.1290, (bf16[2,128,128]{2,1,0:T(8,128)(2,1)S(1)}, ...), branch_computations={%region_64.0_spmd, %region_65.0_spmd, %region_66.0_spmd, %region_6... | conditional | bytes 786536 | solution.py:347
  118.0 5.6 %collective-permute-start.128 = (bf16[2,128,128]{2,1,0:T(8,128)(2,1)S(1)}, bf16[2,128,128]{2,1,0:T(8,128)(2,1)S(1)}, u32[]{:S(2)}, u32[]{:S(2)}) collective-permute-start(bf16[2,128,128]{2,1,0:T(8,128)(2,1)S(1)} %get-tuple-element.664), channel_id=1, source_target_pairs={{0,2},{1,3},{2,4},{3,5},{4,6},{5,7},{6,8},{7,9},{8,10},{9,11},{10,... | collective-permute-start | bytes 196616 | tf_op jit(solution)/shard_map/cond/branch_2_fun/ppermute | solution.py:328
  123.6 9.6 %collective-permute-start.129 = (bf16[2,128,128]{2,1,0:T(8,128)(2,1)S(1)}, bf16[2,128,128]{2,1,0:T(8,128)(2,1)S(1)}, u32[]{:S(2)}, u32[]{:S(2)}) collective-permute-start(bf16[2,128,128]{2,1,0:T(8,128)(2,1)S(1)} %get-tuple-element.665), channel_id=1, source_target_pairs={{2,0},{3,1},{4,2},{5,3},{6,4},{7,5},{8,6},{9,7},{10,8},{11,9},{12,... | collective-permute-start | bytes 196616 | tf_op jit(solution)/shard_map/cond/branch_2_fun/ppermute | solution.py:328
  133.1 1.8 collective-permute-done.128
  135.0 3.2 %collective-permute-done.129 = bf16[2,128,128]{2,1,0:T(8,128)(2,1)S(1)} collective-permute-done((bf16[2,128,128]{2,1,0:T(8,128)(2,1)S(1)}, bf16[2,128,128]{2,1,0:T(8,128)(2,1)S(1)}, u32[]{:S(2)}, u32[]{:S(2)}) %collective-permute-start.129) | collective-permute-done | bytes 65568 | tf_op jit(solution)/shard_map/cond/branch_2_fun/ppermute | solution.py:328
  138.2 0.7 pad_maximum_fusion.1.q
  138.9 0.7 pad_maximum_fusion.u
  139.5 65.6 %shard_map.87 = (bf16[2,2,128,128]{3,2,1,0:T(8,128)(2,1)}, f32[2,2,128,128]{3,2,1,0:T(8,128)}) custom-call(s32[2]{0:T(128)} %order.3, s32[2,2,3]{2,1,0:T(2,128)} %band.3, s32[2,2]{1,0:T(2,128)} %tilt.3, f32[2,2,128,128]{3,2,1,0:T(8,128)} %obj.3, bf16[8,2,128,128]{3,2,1,0:T(8,128)(2,1)} %bank.3, bf16[2,2,128,128]{3,2,1,0:T(8,128)(2,1)} %pad_maximum_fusion.u, ...), custom_call_target="tpu_custom_call" | custom-call | tf_op jit(solution)/shard_map/pallas_call | solution.py:301
  205.2 0.0 copy-start
  205.2 1.6 copy.267
  206.8 0.0 copy-done
  206.8 0.7 copy.268
  (4 shorter events, 0.0 us)
Async XLA Ops:
  73.6 38.3 %collective-permute-start.114 = (bf16[2,128,128]{2,1,0:T(8,128)(2,1)S(1)}, bf16[2,128,128]{2,1,0:T(8,128)(2,1)S(1)}, u32[]{:S(2)}, u32[]{:S(2)}) collective-permute-start(bf16[2,128,128]{2,1,0:T(8,128)(2,1)S(1)} %get-tuple-element.650), channel_id=1, source_target_pairs={{0,226},{1,227},{2,228},{3,229},{4,230},{5,231},{6,232},{7,233},{8... | collective-permute-start | bytes 196616 | tf_op jit(solution)/shard_map/cond/branch_58_fun/ppermute | solution.py:328
  88.2 29.8 %collective-permute-start.115 = (bf16[2,128,128]{2,1,0:T(8,128)(2,1)S(1)}, bf16[2,128,128]{2,1,0:T(8,128)(2,1)S(1)}, u32[]{:S(2)}, u32[]{:S(2)}) collective-permute-start(bf16[2,128,128]{2,1,0:T(8,128)(2,1)S(1)} %get-tuple-element.651), channel_id=1, source_target_pairs={{226,0},{227,1},{228,2},{229,3},{230,4},{231,5},{232,6},{233,7},{2... | collective-permute-start | bytes 196616 | tf_op jit(solution)/shard_map/cond/branch_58_fun/ppermute | solution.py:328
  118.0 17.0 %collective-permute-start.128 = (bf16[2,128,128]{2,1,0:T(8,128)(2,1)S(1)}, bf16[2,128,128]{2,1,0:T(8,128)(2,1)S(1)}, u32[]{:S(2)}, u32[]{:S(2)}) collective-permute-start(bf16[2,128,128]{2,1,0:T(8,128)(2,1)S(1)} %get-tuple-element.664), channel_id=1, source_target_pairs={{0,2},{1,3},{2,4},{3,5},{4,6},{5,7},{6,8},{7,9},{8,10},{9,11},{10,... | collective-permute-start | bytes 196616 | tf_op jit(solution)/shard_map/cond/branch_2_fun/ppermute | solution.py:328
  123.6 14.6 %collective-permute-start.129 = (bf16[2,128,128]{2,1,0:T(8,128)(2,1)S(1)}, bf16[2,128,128]{2,1,0:T(8,128)(2,1)S(1)}, u32[]{:S(2)}, u32[]{:S(2)}) collective-permute-start(bf16[2,128,128]{2,1,0:T(8,128)(2,1)S(1)} %get-tuple-element.665), channel_id=1, source_target_pairs={{2,0},{3,1},{4,2},{5,3},{6,4},{7,5},{8,6},{9,7},{10,8},{11,9},{12,... | collective-permute-start | bytes 196616 | tf_op jit(solution)/shard_map/cond/branch_2_fun/ppermute | solution.py:328
  205.2 1.6 copy-start

commit v2 on v1

--- a/solution.py
+++ b/solution.py
@@ -10,6 +10,7 @@
 
 MESH = pl.DeviceIdType.MESH
 SHIFTS = 8
+VMEM_LIMIT = 16 << 20
 
 
 def left_matrix(bank, index):
@@ -150,7 +151,8 @@
     pl.semaphore_wait(pltpu.get_barrier_semaphore(), number)
 
 
-def first(rows, cols, order, band, tilt, obj, bank, cot, u_out, psi_out, q_out, *scratch):
+def first(rows, cols, order, band, tilt, obj, bank, cot, u_0, u_1, q_0, q_1, psi_out, *scratch):
+    u_out, q_out = (u_0, u_1), (q_0, q_1)
     u_mine, v_mine, h_mine, rim, send, recv = scratch
     width = bank.shape[2]
     greet((("row", rows), ("col", cols)))
@@ -198,7 +200,7 @@
     q += row_term(left_adjoint(bank, band[1, 0, 0]), rim.at[7])
     for angle in range(2):
         for part in range(2):
-            q_out[angle, part] = from_component(q, angle, part).astype(jnp.bfloat16)
+            q_out[angle][part] = from_component(q, angle, part).astype(jnp.bfloat16)
     halo_v.up.wait_recv()
     p += col_term(rim.at[4], right_matrix(bank, band[0, 1, 0]))
     halo_v.down.wait_recv()
@@ -210,14 +212,17 @@
         psi_out[angle, 0] = real
         psi_out[angle, 1] = imag
         real, imag = real.astype(jnp.float32), imag.astype(jnp.float32)
-        u_out[angle, 0] = (s_real * real - s_imag * imag).astype(jnp.bfloat16)
-        u_out[angle, 1] = (s_real * imag + s_imag * real).astype(jnp.bfloat16)
+        u_out[angle][0] = (s_real * real - s_imag * imag).astype(jnp.bfloat16)
+        u_out[angle][1] = (s_real * imag + s_imag * real).astype(jnp.bfloat16)
     for halo in (halo_u, halo_g, halo_v, halo_h):
         halo.wait_send()
 
 
-def second(rows, cols, order, band, tilt, obj, bank, u, q, psi, exit_out, grad_out, *scratch):
-    g_mine, v_mine, h_mine, rim, send, recv = scratch
+def second(rows, cols, order, band, tilt, obj, bank, u_0, u_1, q_0, q_1, psi, exit_out, grad_out, *scratch):
+    g_mine, v_mine, h_mine, rim, send, recv, u = scratch
+    q = (q_0, q_1)
+    u[0] = u_0[...]
+    u[1] = u_1[...]
     width = bank.shape[2]
     greet((("row", rows), ("col", cols)))
     row_start = lax.axis_index("row") * width
@@ -227,7 +232,7 @@
     last_real = None
     last_imag = None
     for angle in range(2):
-        q_real, q_imag = q[angle, 0].astype(jnp.float32), q[angle, 1].astype(jnp.float32)
+        q_real, q_imag = q[angle][0].astype(jnp.float32), q[angle][1].astype(jnp.float32)
         g_mine[angle, 0] = (q_real * s_real + q_imag * s_imag).astype(jnp.bfloat16)
         g_mine[angle, 1] = (q_imag * s_real - q_real * s_imag).astype(jnp.bfloat16)
         real, imag = psi[angle, 0].astype(jnp.float32), psi[angle, 1].astype(jnp.float32)
@@ -310,30 +315,64 @@
             pltpu.VMEM((8, *field), jnp.bfloat16),
             pltpu.SemaphoreType.DMA((8,)),
             pltpu.SemaphoreType.DMA((8,)),
-        ],
-        compiler_params=pltpu.CompilerParams(collective_id=number, has_side_effects=True),
+        ]
+        + [pltpu.VMEM(field, jnp.bfloat16)] * number,
+        compiler_params=pltpu.CompilerParams(
+            collective_id=number, has_side_effects=True, vmem_limit_bytes=VMEM_LIMIT
+        ),
     )(*arrays)
+
+
+def swap(row_step, col_step, rows, cols, u, q, u_out, q_out, send, recv):
+    row, col = lax.axis_index("row"), lax.axis_index("col")
+    ahead = (lax.rem(row + row_step, rows), lax.rem(col + col_step, cols))
+    behind = (lax.rem(row + rows - row_step, rows), lax.rem(col + cols - col_step, cols))
+    barrier = pltpu.get_barrier_semaphore()
+    for other in (ahead, behind):
+        pl.semaphore_signal(barrier, inc=1, device_id=other, device_id_type=MESH)
+    met(2)
+    copies = [
+        pltpu.make_async_remote_copy(
+            src_ref=source,
+            dst_ref=target,
+            send_sem=send.at[slot],
+            recv_sem=recv.at[slot],
+            device_id=other,
+            device_id_type=MESH,
+        )
+        for slot, (source, target, other) in enumerate(((u, u_out, ahead), (q, q_out, behind)))
+    ]
+    for copy in copies:
+        copy.start()
+    for copy in copies:
+        copy.wait()
 
 
 def move(row_step, col_step, rows, cols, u, q):
     if row_step == 0 and col_step == 0:
         return u, q
-    there = []
-    for row in range(rows):
-        for col in range(cols):
-            target = (row + row_step) % rows * cols + (col + col_step) % cols
-            there.append((row * cols + col, target))
-    back = [(target, source) for source, target in there]
-    axes = ("row", "col")
-    return lax.ppermute(u, axes, there), lax.ppermute(q, axes, back)
+    vmem = pl.BlockSpec(memory_space=pltpu.VMEM)
+    return pl.pallas_call(
+        functools.partial(swap, row_step, col_step, rows, cols),
+        out_shape=[jax.ShapeDtypeStruct(u.shape, u.dtype)] * 2,
+        in_specs=[vmem] * 2,
+        out_specs=[vmem] * 2,
+        scratch_shapes=[pltpu.SemaphoreType.DMA((2,)), pltpu.SemaphoreType.DMA((2,))],
+        compiler_params=pltpu.CompilerParams(
+            collective_id=1 + row_step * SHIFTS + col_step,
+            has_side_effects=True,
+            vmem_limit_bytes=VMEM_LIMIT,
+        ),
+    )(u, q)
 
 
 def local(rows, cols, obj, bank, band_index, tilt, tile_shift, slice_order, cot):
     width = bank.shape[2]
-    small = jax.ShapeDtypeStruct(cot.shape, jnp.bfloat16)
-    u, psi, q = call(
+    field = jax.ShapeDtypeStruct(cot.shape, jnp.bfloat16)
+    part = jax.ShapeDtypeStruct(cot.shape[1:], jnp.bfloat16)
+    u_0, u_1, q_0, q_1, psi = call(
         functools.partial(first, rows, cols),
-        (small, small, small),
+        (part, part, part, part, field),
         (slice_order, band_index, tilt, obj, bank, cot),
         width,
         0,
@@ -344,13 +383,12 @@
         for row_step in range(SHIFTS)
         for col_step in range(SHIFTS)
     ]
-    moved = [lax.switch(choice[angle], branches, u[angle], q[angle]) for angle in range(2)]
-    u = jnp.stack([moved[0][0], moved[1][0]])
-    q = jnp.stack([moved[0][1], moved[1][1]])
+    u_0, q_0 = lax.switch(choice[0], branches, u_0, q_0)
+    u_1, q_1 = lax.switch(choice[1], branches, u_1, q_1)
     exit_field, grad = call(
         functools.partial(second, rows, cols),
-        (small, jax.ShapeDtypeStruct(obj.shape, jnp.float32)),
-        (slice_order, band_index, tilt, obj, bank, u, q, psi),
+        (field, jax.ShapeDtypeStruct(obj.shape, jnp.float32)),
+        (slice_order, band_index, tilt, obj, bank, u_0, u_1, q_0, q_1, psi),
         width,
         1,
     )

time: 208 us -> 203 us (0.976)
  Pallas kernels: 135 us -> 194 us
  starting transfers between devices: 53.4 us -> 0 us
  waiting for transfers between devices: 11.1 us -> 0 us
    pallas_call x0 -> x2, Pallas kernels: none -> 61.9 us  [move(): pl.pallas_call(functools.partial(swap, row_step, col_step, rows, cols), o...]
    ppermute x4 -> x0, starting transfers between devices: 53.4 us -> none  [move(): return (lax.ppermute(u, axes, there), lax.ppermute(q, axes, back))]
    ppermute x4 -> x0, waiting for transfers between devices: 11.1 us -> none  [move(): return (lax.ppermute(u, axes, there), lax.ppermute(q, axes, back))]
    unnamed x4 -> x18, local copies, waits for them, and re-layouts: 2.32 us -> 4.93 us
    pallas_call x2, Pallas kernels: 135 us -> 133 us  [call(): pl.pallas_call(body, out_shape=outs, in_specs=[smem] * 3 + [vmem] * (len(...]
  transfers between devices with their start and end apart: 4 -> 0, of which waited for: 3 -> 0; matrix products, arithmetic and copies ran while one was open for 0% -> 0% of each run, Pallas kernels for 0% -> 0%
where the time goes in v2:
time: 203 us
  Pallas kernels  194 us (96%)
  local copies, waits for them, and re-layouts  5.48 us (3%)
  between operations  2.05 us (1%)
    pallas_call x2, Pallas kernels, call(): pl.pallas_call(body, out_shape=outs, in_specs=[smem] * 3 + [vmem] * (len(...  133 us
    pallas_call x2, Pallas kernels, move(): pl.pallas_call(functools.partial(swap, row_step, col_step, rows, cols), o...  61.9 us
    unnamed x18, local copies, waits for them, and re-layouts  4.93 us

profile of v2, /device:TPU:71, one launch (start us, length us, event | category | flops | bytes accessed | tf_op | source)
XLA Modules:
  0.0 203.0 jit_solution(14456656257058969465)
XLA Ops:
  0.6 0.8 slice_add_fusion
  1.5 0.5 fusion
  2.6 0.0 copy-start.5
  3.3 0.0 copy-start.6
  3.3 0.0 copy-start.7
  3.3 0.0 copy-done.5
  3.3 0.6 copy-done.6
  4.0 0.0 copy-done.7
  4.0 0.0 copy-start
  4.0 1.0 copy-done
  5.0 0.0 copy-start.2
  5.0 0.9 copy-done.2
  6.0 0.0 copy-start.4
  6.0 0.9 copy-done.4
  6.9 68.0 %shard_map.86 = (bf16[2,128,128]{2,1,0:T(8,128)(2,1)S(1)}, bf16[2,128,128]{2,1,0:T(8,128)(2,1)S(1)}, bf16[2,128,128]{2,1,0:T(8,128)(2,1)S(1)}, bf16[2,128,128]{2...) custom-call(s32[2]{0:T(128)S(1)} %copy-done.7, s32[2,2,3]{2,1,0:T(2,128)S(1)} %copy-done.5, s32[2,2]{1,0:T(2,128)S(1)} %copy-done.6, ...), custom_call_target="tpu_custom_call" | custom-call | tf_op jit(solution)/shard_map/pallas_call | solution.py:306
  74.9 36.9 %conditional.2 = ((bf16[2,128,128]{2,1,0:T(8,128)(2,1)S(1)}, bf16[2,128,128]{2,1,0:T(8,128)(2,1)S(1)})) conditional(s32[]{:T(128)} %bitcast, (bf16[2,128,128]{2,1,0:T(8,128)(2,1)S(1)}, bf16[2,128,128]{2,1,0:T(8,128)(2,1)S(1)}) %tuple.391, (bf16[2,128,128]{2,1,0:T(8,128)(2,1)S(1)}, ...), branch_computations={%region_0.0_spmd, %region_1.0_spmd, %region_2.0_spmd, %region_3.0_... | conditional | bytes 262152 | solution.py:386
  75.0 36.8 %branch_47_fun.2 = (bf16[2,128,128]{2,1,0:T(8,128)(2,1)S(1)}, bf16[2,128,128]{2,1,0:T(8,128)(2,1)S(1)}) custom-call(bf16[2,128,128]{2,1,0:T(8,128)(2,1)S(1)} %copy.611.u, bf16[2,128,128]{2,1,0:T(8,128)(2,1)S(1)} %copy.612.q), custom_call_target="tpu_custom_call" | custom-call | tf_op jit(solution)/shard_map/cond/branch_47_fun/pallas_call | solution.py:355
  111.8 0.0 copy-start.1
  111.8 0.0 copy-start.3
  111.8 25.3 %conditional.3 = ((bf16[2,128,128]{2,1,0:T(8,128)(2,1)S(1)}, bf16[2,128,128]{2,1,0:T(8,128)(2,1)S(1)})) conditional(s32[]{:T(128)} %bitcast.1, (bf16[2,128,128]{2,1,0:T(8,128)(2,1)S(1)}, bf16[2,128,128]{2,1,0:T(8,128)(2,1)S(1)}) %tuple.392, (bf16[2,128,128]{2,1,0:T(8,128)(2,1)S(1)}, ...), branch_computations={%region_64.0_spmd, %region_65.0_spmd, %region_66.0_spmd, %region_6... | conditional | bytes 262152 | solution.py:387
  111.9 25.1 %branch_48_fun.3 = (bf16[2,128,128]{2,1,0:T(8,128)(2,1)S(1)}, bf16[2,128,128]{2,1,0:T(8,128)(2,1)S(1)}) custom-call(bf16[2,128,128]{2,1,0:T(8,128)(2,1)S(1)} %copy.739.u, bf16[2,128,128]{2,1,0:T(8,128)(2,1)S(1)} %copy.740.q), custom_call_target="tpu_custom_call" | custom-call | tf_op jit(solution)/shard_map/cond/branch_48_fun/pallas_call | solution.py:355
  137.1 0.0 copy-done.1
  137.1 0.0 copy-done.3
  137.1 64.5 %shard_map.87 = (bf16[2,2,128,128]{3,2,1,0:T(8,128)(2,1)S(1)}, f32[2,2,128,128]{3,2,1,0:T(8,128)S(1)}) custom-call(s32[2]{0:T(128)S(1)} %copy-done.7, s32[2,2,3]{2,1,0:T(2,128)S(1)} %copy-done.5, s32[2,2]{1,0:T(2,128)S(1)} %copy-done.6, f32[2,2,128,128]{3,2,1,0:T(8,128)S(1)} %copy-done.3, bf16[8,2,128,128]{3,2,1,0:T(8,128)(2,1)S(1)} %copy-done.1, ...), custom_call_target="tpu_custom_call" | custom-call | tf_op jit(solution)/shard_map/pallas_call | solution.py:306
  201.6 0.7 copy.771
  202.3 0.7 copy.772
  (4 shorter events, 0.0 us)
Async XLA Ops:
  2.6 0.7 copy-start.5
  3.3 0.7 copy-start.6
  3.3 0.7 copy-start.7
  4.0 1.0 copy-start
  5.0 0.9 copy-start.2
  6.0 0.9 copy-start.4
  111.8 25.3 %copy-start.1 = (bf16[8,2,128,128]{3,2,1,0:T(8,128)(2,1)S(1)}, bf16[8,2,128,128]{3,2,1,0:T(8,128)(2,1)}, u32[]{:S(2)}) copy-start(bf16[8,2,128,128]{3,2,1,0:T(8,128)(2,1)} %bank.3) | copy-start | bytes 1572868
  111.8 25.3 %copy-start.3 = (f32[2,2,128,128]{3,2,1,0:T(8,128)S(1)}, f32[2,2,128,128]{3,2,1,0:T(8,128)}, u32[]{:S(2)}) copy-start(f32[2,2,128,128]{3,2,1,0:T(8,128)} %obj.3) | copy-start | bytes 786436
